TPU v7x, 32 devices: a whole 2x2x4 slice. The times are simulated.
32 devices in a mesh: region: 4 (over y, x), col: 8 (over z, core).
Axes of the slice: x: 2, y: 2, z: 4, core: 2. Of those that a mesh axis runs over, the one named last changes fastest.
Arguments:
- jac: bfloat16 [256, 128], P(('region', 'col')), may hold values from -2 to 2
- dest: int32 [256, 2], P(('region', 'col')), may hold values from 0 to 3, all different within a row; in each aligned block of 8 rows (0 to 7, 8 to 15, ...) at most 6 rows name the same one
- near_pose: int32 [256, 2], P(('region', 'col')), may hold values from 0 to 255
- prior: float32 [8192], P('region'), may hold values from 0.5 to 8
Outputs:
- front_out: float32 [8192, 8192], P('region', 'col')
Inputs may be any that keep to these rules, and one draw needn't show every extreme that they name: `dest`: each row names two different regions; among the 8 rows of one device no region is named more than 6 times, and in some device's rows some region is named exactly 6 times.
All inputs are finite; a program needn't handle non-finite values.
Results may differ from a plain program's by a relative error of at most 0.00045.
Values may be sent and summed in bfloat16 or wider, within the bound.
No kernel may reach another device: no remote copies, remote signals or barrier semaphores. Data moves between devices by JAX's collectives and lax.ppermute only.
A program may use at most 320 MiB of HBM per device.

v0:
```python
import jax
import jax.numpy as jnp
from jax import lax
from jax.sharding import PartitionSpec as P

NB = 128
K_PANELS = 2


def broadcast(block, axis, owner):
    block = jnp.where(lax.axis_index(axis) == owner, block, jnp.zeros_like(block))
    return lax.psum(block, axis)


def placed(pose_pair, blocks, first_pose, pose_count):
    pose_grid = first_pose + jnp.arange(pose_count, dtype=jnp.int32)
    summed = jnp.zeros((blocks.shape[0], 8, pose_count, 8), jnp.float32)
    for endpoint in range(2):
        matches = (pose_pair[:, endpoint][:, None] == pose_grid[None, :]).astype(jnp.float32)
        summed = summed + matches[:, None, :, None] * blocks[:, endpoint][:, :, None, :]
    return summed.astype(jnp.bfloat16).reshape(blocks.shape[0] * 8, pose_count * 8)


def body(jac, dest, near_pose, prior):
    regions = lax.axis_size("region")
    columns = lax.axis_size("col")
    region_index = lax.axis_index("region")
    column_index = lax.axis_index("col")
    count_rows = jac.shape[0]
    row_block = prior.shape[0]
    front = row_block * regions
    col_block = front // columns
    region_poses = front // 8 // regions
    capacity = max(2, 3 * count_rows // regions)
    slots_out = regions * capacity
    targets = dest.reshape(-1)
    member = (targets[:, None] == jnp.arange(regions, dtype=jnp.int32)[None, :]).astype(jnp.int32)
    ranking = jnp.sum(jnp.cumsum(member, axis=0) * member, axis=1) - 1
    position = targets * capacity + ranking
    placing = (position[None, :] == jnp.arange(slots_out, dtype=jnp.int32)[:, None]).astype(
        jnp.bfloat16
    )
    copies = jnp.repeat(jac, 2, axis=0)
    labels = jnp.concatenate([near_pose // 64, near_pose % 64, dest], axis=1).astype(jnp.bfloat16)
    label_copies = jnp.repeat(labels, 2, axis=0)
    packed = (
        jnp.dot(placing, copies, preferred_element_type=jnp.float32)
        .astype(jnp.bfloat16)
        .reshape(regions, capacity, 128)
    )
    packed_labels = (
        jnp.dot(placing, label_copies, preferred_element_type=jnp.float32)
        .astype(jnp.bfloat16)
        .reshape(regions, capacity, 6)
    )
    arrived, arrived_labels = (
        lax.all_to_all(packed, "region", split_axis=0, concat_axis=0, tiled=True),
        lax.all_to_all(packed_labels, "region", split_axis=0, concat_axis=0, tiled=True),
    )
    piece_rows = lax.all_gather(arrived, "col", axis=0, tiled=True)
    piece_labels = lax.all_gather(arrived_labels, "col", axis=0, tiled=True)
    slot_count = piece_rows.shape[0] * piece_rows.shape[1]
    blocks = piece_rows.reshape(slot_count, 2, 8, 8).astype(jnp.float32)
    label_values = piece_labels.reshape(slot_count, 6).astype(jnp.int32)
    near_values = label_values[:, 0:2] * 64 + label_values[:, 2:4]
    pose_pair = label_values[:, 4:6] * region_poses + near_values
    own_rows = placed(pose_pair, blocks, region_index * region_poses, region_poses)
    own_cols = placed(pose_pair, blocks, column_index * (col_block // 8), col_block // 8)
    matrix = lax.dot_general(
        own_rows, own_cols, (((0,), (0,)), ((), ())), preferred_element_type=jnp.float32
    )
    row_global = region_index * row_block + jnp.arange(row_block, dtype=jnp.int32)
    col_global = column_index * col_block + jnp.arange(col_block, dtype=jnp.int32)
    matrix = matrix + jnp.where(row_global[:, None] == col_global[None, :], prior[:, None], 0.0)
    for panel_number in range(K_PANELS):
        low_edge = panel_number * NB
        high_edge = low_edge + NB
        owner_col = low_edge // col_block
        offset_col = low_edge - owner_col * col_block
        local_panel = lax.slice_in_dim(matrix, offset_col, offset_col + NB, axis=1)
        panel_part = broadcast(local_panel.astype(jnp.bfloat16), "col", owner_col).astype(
            local_panel.dtype
        )
        whole_panel = lax.all_gather(
            panel_part.astype(jnp.bfloat16), "region", axis=0, tiled=True
        ).astype(panel_part.dtype)
        diagonal = lax.slice_in_dim(whole_panel, low_edge, high_edge, axis=0)
        their_rows = lax.dynamic_slice_in_dim(
            whole_panel, column_index * col_block, col_block, axis=0
        )
        factor = jnp.tril(jnp.linalg.cholesky(diagonal))
        panel_cols = low_edge + jnp.arange(NB, dtype=jnp.int32)

        def finish(block_rows, global_rows):
            solved = jax.scipy.linalg.solve_triangular(factor, block_rows.T, lower=True).T
            keeping = global_rows[:, None] >= panel_cols[None, :]
            return jnp.where(keeping, solved, 0.0)

        mine = finish(panel_part, row_global)
        theirs = finish(their_rows, col_global)
        matrix = matrix - jnp.dot(mine, theirs.T, precision=lax.Precision.HIGHEST)
        with_panel = matrix.at[:, offset_col : offset_col + NB].set(mine)
        matrix = jnp.where(column_index == owner_col, with_panel, matrix)
        in_panel = (row_global >= low_edge) & (row_global < high_edge)
        right_side = col_global >= high_edge
        matrix = jnp.where(in_panel[:, None] & right_side[None, :], 0.0, matrix)
    return matrix


def solution(mesh):
    return jax.shard_map(
        body,
        mesh=mesh,
        in_specs=(
            P(("region", "col"), None),
            P(("region", "col"), None),
            P(("region", "col"), None),
            P("region"),
        ),
        out_specs=P("region", "col"),
        check_vma=False,
    )
```

profile of v0, /device:TPU:0, one launch (start us, length us, event | category | flops | bytes accessed | tf_op | source)
XLA Modules:
  0.0 640.7 jit_solution(2428502559729770655)
XLA Ops:
  6.5 0.8 copy.32
  7.3 0.7 convert.21
  8.4 0.7 fusion.41
  10.1 5.2 all-to-all-start
  16.0 3.9 all-to-all-done
  19.9 3.2 all-to-all-start.1
  23.4 14.2 %all_gather.12 = bf16[32,6,6]{2,1,0:T(8,128)(2,1)S(1)} all-gather(bf16[4,6,6]{2,1,0:T(8,128)(2,1)S(1)} %copy.35), channel_id=1, replica_groups=mesh['region'=4,'col'=8] {'col'}, dimensions={0}, use_global_device_ids=true | all-gather | bytes 2592 | tf_op jit(solution)/shard_map/all_gather | solution.py:61
  38.1 0.8 compare_convert_fusion.3
  38.9 14.0 %all_gather.13 = bf16[32,6,128]{2,1,0:T(8,128)(2,1)S(1)} all-gather(bf16[4,6,128]{2,1,0:T(8,128)(2,1)S(1)} %all-to-all-done.1), channel_id=1, replica_groups=mesh['region'=4,'col'=8] {'col'}, dimensions={0}, use_global_device_ids=true | all-gather | bytes 55296 | tf_op jit(solution)/shard_map/all_gather | solution.py:60
  52.9 0.8 reshape.294
  53.9 43.1 %add_convert_fusion = bf16[192,8,256,8]{3,2,1,0:T(8,128)(2,1)} fusion(f32[192,8,8]{2,1,0:T(8,128)S(1)} %get-tuple-element.33, f32[192,256]{1,0:T(8,128)S(1)} %get-tuple-element.37, f32[192,8,8]{2,1,0:T(8,128)S(1)} %get-tuple-element.32, f32[192,256]{1,0:T(8,128)S(1)} %get-tuple-element.36), kind=kLoop, calls=%fused_computation | loop fusion | flops 12582912 | bytes 6782976 | tf_op jit(solution)/shard_map/convert_element_type | solution.py:21
  96.9 141.8 %convert_element_type.99 = bf16[1536,2048]{1,0:T(8,128)(2,1)} reshape(bf16[192,8,256,8]{3,2,1,0:T(8,128)(2,1)} %add_convert_fusion) | data formatting | bytes 12582912 | tf_op jit(solution)/shard_map/convert_element_type | solution.py:21
  238.7 23.6 %add_convert_fusion.1 = bf16[192,8,128,8]{3,2,1,0:T(8,128)(2,1)} fusion(f32[192,8,8]{2,1,0:T(8,128)S(1)} %get-tuple-element.33, f32[192,128]{1,0:T(8,128)S(1)} %copy-done.9, f32[192,8,8]{2,1,0:T(8,128)S(1)} %get-tuple-element.32, f32[192,128]{1,0:T(8,128)S(1)} %copy-done.8), kind=kLoop, calls=%fused_computation.1 | loop fusion | flops 6291456 | bytes 3440640 | tf_op jit(solution)/shard_map/convert_element_type | solution.py:21
  262.3 71.0 %convert_element_type.103 = bf16[1536,1024]{1,0:T(8,128)(2,1)S(1)} reshape(bf16[192,8,128,8]{3,2,1,0:T(8,128)(2,1)} %add_convert_fusion.1) | data formatting | bytes 6291456 | tf_op jit(solution)/shard_map/convert_element_type | solution.py:21
  333.3 9.5 %select_add_fusion = f32[2048,1024]{0,1:T(8,128)S(1)} fusion(f32[2048]{0:T(1024)S(1)} %copy-done.10, s32[2048]{0:T(1024)S(1)} %iota_add_fusion, s32[1024]{0:T(1024)S(1)} %iota_add_fusion.1, bf16[1536,2048]{1,0:T(8,128)(2,1)} %convert_element_type.99, bf16[1536,1024]{1,0:T(8,128)(2,1)S(1)} %convert_element_type.103), kind=kOutput, calls=%fused_computation.2 | convolution fusion | flops 6448742400 | bytes 17846272 | tf_op jit(solution)/shard_map/dot_general | solution.py:69
  342.8 3.4 copy-done.3
  346.2 0.8 fusion.10
  347.1 58.0 %all-reduce.3.cloned.1.call-done = bf16[2048,128]{0,1:T(8,128)(2,1)} async-done(((bf16[2048,128]{0,1:T(8,128)(2,1)}), bf16[2048,128]{0,1:T(8,128)(2,1)}) %all-reduce.3.cloned.1.call-update) | async-done | bytes 524304 | tf_op jit(solution)/shard_map/psum | solution.py:12
  406.0 35.2 %all-gather.3.cloned.1.call-done = bf16[8192,128]{0,1:T(8,128)(2,1)} async-done(((bf16[2048,128]{0,1:T(8,128)(2,1)}), bf16[8192,128]{0,1:T(8,128)(2,1)}) %all-gather.3.cloned.1.call-update) | async-done | bytes 2097168 | tf_op jit(solution)/shard_map/all_gather | solution.py:84
  441.2 0.8 slice.110
  442.1 2.0 convert_element_type.104
  444.1 1.9 copy-done.5
  446.1 11.7 %cholesky.44 = f32[128,128]{1,0:T(8,128)S(1)} custom-call(f32[128,128]{1,0:T(8,128)S(1)} %fusion.25), custom_call_target="Cholesky" | custom-call | tf_op jit(solution)/shard_map/jit(cholesky)/cholesky | solution.py:91
  457.8 0.7 compare_reduce_fusion.1
  458.5 0.6 fusion.18
  459.2 9.8 %custom-call.10 = f32[1,128,128]{1,2,0:T(8,128)S(1)} custom-call(f32[1,128,128]{2,1,0:T(8,128)S(1)} %fusion.18), custom_call_target="InvertDiagBlocksLowerTriangular" | custom-call | tf_op jit(solution)/shard_map/jit(_solve_triangular)/triangular_solve | solution.py:95
  469.0 1.7 fusion.3
  470.7 1.1 fusion.1
  471.8 9.4 %convolution_subtract_fusion.1 = f32[2048,1024]{0,1:T(8,128)S(1)} fusion(f32[2048,1024]{0,1:T(8,128)} %copy-done.3, f32[2048,128]{0,1:T(8,128)S(1)} %fusion.1, f32[1024,128]{0,1:T(8,128)S(1)} %fusion.3), kind=kOutput, calls=%fused_computation.6 | convolution fusion | flops 3223322624 | bytes 18350080 | tf_op jit(solution)/shard_map/dot_general | solution.py:101
  481.1 0.9 fusion.4
  482.0 0.9 and_select_fusion
  482.9 3.4 copy-done.2
  486.3 0.8 fusion.11
  487.2 56.6 %all-reduce.5.cloned.1.call-done = bf16[2048,128]{0,1:T(8,128)(2,1)} async-done(((bf16[2048,128]{0,1:T(8,128)(2,1)}), bf16[2048,128]{0,1:T(8,128)(2,1)}) %all-reduce.5.cloned.1.call-update) | async-done | bytes 524304 | tf_op jit(solution)/shard_map/psum | solution.py:12
  544.6 35.3 %all-gather.5.cloned.1.call-done = bf16[8192,128]{0,1:T(8,128)(2,1)} async-done(((bf16[2048,128]{0,1:T(8,128)(2,1)}), bf16[8192,128]{0,1:T(8,128)(2,1)}) %all-gather.5.cloned.1.call-update) | async-done | bytes 2097168 | tf_op jit(solution)/shard_map/all_gather | solution.py:84
  579.9 0.8 slice.113
  580.7 2.0 convert_element_type.105
  582.7 1.9 copy-done.4
  584.7 11.7 %cholesky.55 = f32[128,128]{1,0:T(8,128)S(1)} custom-call(f32[128,128]{1,0:T(8,128)S(1)} %fusion.22), custom_call_target="Cholesky" | custom-call | tf_op jit(solution)/shard_map/jit(cholesky)/cholesky | solution.py:91
  596.4 0.7 compare_reduce_fusion
  597.1 0.6 fusion.19
  597.8 9.8 %custom-call.12 = f32[1,128,128]{1,2,0:T(8,128)S(1)} custom-call(f32[1,128,128]{2,1,0:T(8,128)S(1)} %fusion.19), custom_call_target="InvertDiagBlocksLowerTriangular" | custom-call | tf_op jit(solution)/shard_map/jit(_solve_triangular)/triangular_solve | solution.py:95
  607.6 1.7 fusion.2
  609.3 1.1 fusion
  610.4 9.2 %convolution_subtract_fusion = f32[2048,1024]{0,1:T(8,128)S(1)} fusion(f32[2048,1024]{0,1:T(8,128)} %copy-done.2, f32[2048,128]{0,1:T(8,128)S(1)} %fusion, f32[1024,128]{0,1:T(8,128)S(1)} %fusion.2), kind=kOutput, calls=%fused_computation.5 | convolution fusion | flops 3223322624 | bytes 18350080 | tf_op jit(solution)/shard_map/dot_general | solution.py:101
  619.5 0.9 fusion.5
  620.4 4.1 and_select_fusion.1
  624.5 9.2 %copy.43 = f32[2048,1024]{1,0:T(8,128)} copy(f32[2048,1024]{0,1:T(8,128)} %and_select_fusion.1) | data formatting | bytes 16777216 | tf_op jit(solution)/shard_map/jit(_where)/select_n | solution.py:106
  (67 shorter events, 4.9 us)
Async XLA Ops:
  6.5 8.7 %copy-start = (bf16[8,128]{1,0:T(8,128)(2,1)S(1)}, bf16[8,128]{1,0:T(8,128)(2,1)}, u32[]{:S(2)}) copy-start(bf16[8,128]{1,0:T(8,128)(2,1)} %param.13) | copy-start | bytes 6148
  10.1 9.9 %all-to-all-start = ((bf16[4,6,6]{1,2,0:T(8,128)(2,1)}), bf16[4,6,6]{1,2,0:T(8,128)(2,1)S(1)}, u32[]{:S(2)}, u32[]{:S(2)}) async-start(bf16[4,6,6]{1,2,0:T(8,128)(2,1)} %copy.34), calls=%async_computation | async-start | bytes 16384 | tf_op jit(solution)/shard_map/all_to_all | solution.py:58
  19.9 19.0 %all-to-all-start.1 = ((bf16[4,6,128]{2,1,0:T(8,128)(2,1)}), bf16[4,6,128]{2,1,0:T(8,128)(2,1)S(1)}, u32[]{:S(2)}, u32[]{:S(2)}) async-start(bf16[4,6,128]{2,1,0:T(8,128)(2,1)} %reshape.292), calls=%async_computation.1 | async-start | bytes 16384 | tf_op jit(solution)/shard_map/all_to_all | solution.py:57
  23.2 381.9 %all-reduce.3.cloned.1.call-start = ((), (), s32[]{:S(2)}) async-start(), calls=%async_computation.2 | async-start | bytes 1048576 | tf_op jit(solution)/shard_map/psum | solution.py:12
  96.9 141.8 %copy-start.8 = (f32[192,128]{1,0:T(8,128)S(1)}, f32[192,128]{1,0:T(8,128)}, u32[]{:S(2)}) copy-start(f32[192,128]{1,0:T(8,128)} %get-tuple-element.40) | copy-start | bytes 294916
  96.9 141.8 %copy-start.9 = (f32[192,128]{1,0:T(8,128)S(1)}, f32[192,128]{1,0:T(8,128)}, u32[]{:S(2)}) copy-start(f32[192,128]{1,0:T(8,128)} %get-tuple-element.41) | copy-start | bytes 294916
  262.3 71.0 %copy-start.10 = (f32[2048]{0:T(1024)S(1)}, f32[2048]{0:T(1024)}, u32[]{:S(2)}) copy-start(f32[2048]{0:T(1024)} %param.16) | copy-start | bytes 24580
  342.8 3.4 copy-start.3
  347.1 94.2 %all-gather.3.cloned.1.call-start = ((), (), s32[]{:S(2)}) async-start(), calls=%async_computation.3 | async-start | bytes 2621440 | tf_op jit(solution)/shard_map/all_gather | solution.py:84
  405.1 65.5 %copy-start.6 = (bf16[2048,128]{0,1:T(8,128)(2,1)S(1)}, bf16[2048,128]{0,1:T(8,128)(2,1)}, u32[]{:S(2)}) copy-start(bf16[2048,128]{0,1:T(8,128)(2,1)} %all-reduce.3.cloned.1.call-done) | copy-start | bytes 1572868
  405.2 138.7 %all-reduce.5.cloned.1.call-start = ((), (), s32[]{:S(2)}) async-start(), calls=%async_computation.4 | async-start | bytes 1048576 | tf_op jit(solution)/shard_map/psum | solution.py:12
  444.1 1.9 copy-start.5
  482.9 3.4 copy-start.2
  487.2 92.7 %all-gather.5.cloned.1.call-start = ((), (), s32[]{:S(2)}) async-start(), calls=%async_computation.5 | async-start | bytes 2621440 | tf_op jit(solution)/shard_map/all_gather | solution.py:84
  543.9 65.4 %copy-start.7 = (bf16[2048,128]{0,1:T(8,128)(2,1)S(1)}, bf16[2048,128]{0,1:T(8,128)(2,1)}, u32[]{:S(2)}) copy-start(bf16[2048,128]{0,1:T(8,128)(2,1)} %all-reduce.5.cloned.1.call-done) | copy-start | bytes 1572868
  582.7 1.9 copy-start.4
  620.4 13.4 %copy-start.1 = (bf16[8,128]{1,0:T(8,128)(2,1)S(1)}, bf16[8,128]{1,0:T(8,128)(2,1)}, u32[]{:S(2)}) copy-start(bf16[8,128]{1,0:T(8,128)(2,1)} %param.13) | copy-start | bytes 6148
Sparse Core Ops, SparseCore 0:
  347.2 57.9 all-reduce.2
  407.0 34.2 all-gather.2
  487.3 56.5 all-reduce.4
  545.6 34.2 all-gather.4
where the time goes:
time: 649 us; the launch traced here: 641 us
  local copies, waits for them, and re-layouts  238 us (37%)
  waiting for transfers between devices  189 us (29%)
  other arithmetic  129 us (20%)
  matrix products  33.8 us (5%)
  blocking collectives  28.2 us (4%)
  between operations  13.8 us (2%)
  starting transfers between devices  8.78 us (1%)
    convert_element_type x2, local copies, waits for them, and re-layouts, placed(): summed.astype(jnp.bfloat16).reshape(blocks.shape[0] * 8, pose_count * 8)  213 us
    psum x2, waiting for transfers between devices, broadcast(): return lax.psum(block, axis)  115 us
    all_gather x2, waiting for transfers between devices, body(): lax.all_gather(panel_part.astype(jnp.bfloat16), 'region', axis=0, tiled=T...  70.5 us
    convert_element_type x2, other arithmetic, placed(): summed.astype(jnp.bfloat16).reshape(blocks.shape[0] * 8, pose_count * 8)  66.7 us
    another operation x6, other arithmetic, body(): factor = jnp.tril(jnp.linalg.cholesky(diagonal))  24.9 us
    another operation x4, other arithmetic, finish(): jax.scipy.linalg.solve_triangular(factor, block_rows.T, lower=True)  20.9 us
    dot_general x2, matrix products, body(): matrix = matrix - jnp.dot(mine, theirs.T, precision=lax.Precision.HIGHEST)  18.5 us
    all_gather x1, blocking collectives, body(): piece_labels = lax.all_gather(arrived_labels, 'col', axis=0, tiled=True)  14.2 us
  transfers between devices with their start and end apart: 6, of which 5 were waited for; matrix products, arithmetic and copies ran while one was open for 1% of the time, Pallas kernels for 0%

commit v1 on v0

--- a/solution.py
+++ b/solution.py
@@ -1,3 +1,4 @@
+import functools
 import jax
 import jax.numpy as jnp
 from jax import lax
@@ -5,6 +6,30 @@
 
 NB = 128
 K_PANELS = 2
+
+
+def get_node(my_data, axis_k):
+    later = lax.axis_size("region")
+    row_out = lax.axis_index("region")
+    reply, piece_now, inter = (later, row_out, my_data.shape[axis_k])
+    arr_out, fresh = (my_data, 1)
+    while fresh < reply:
+        arr_out = jnp.concatenate(
+            [
+                arr_out,
+                lax.ppermute(
+                    arr_out,
+                    axis_name="region",
+                    perm=[(ii, (ii - fresh) % reply) for ii in range(reply)],
+                ),
+            ],
+            axis_k,
+        )
+        fresh = 2 * fresh
+    return jnp.roll(arr_out, piece_now * inter, axis=axis_k)
+
+
+_list_limits = functools.partial(get_node, axis_k=0)
 
 
 def broadcast(block, axis, owner):
@@ -81,9 +106,7 @@
         panel_part = broadcast(local_panel.astype(jnp.bfloat16), "col", owner_col).astype(
             local_panel.dtype
         )
-        whole_panel = lax.all_gather(
-            panel_part.astype(jnp.bfloat16), "region", axis=0, tiled=True
-        ).astype(panel_part.dtype)
+        whole_panel = _list_limits(panel_part.astype(jnp.bfloat16)).astype(panel_part.dtype)
         diagonal = lax.slice_in_dim(whole_panel, low_edge, high_edge, axis=0)
         their_rows = lax.dynamic_slice_in_dim(
             whole_panel, column_index * col_block, col_block, axis=0

time: 649 us -> 653 us (level)
  waiting for transfers between devices: 189 us -> 180 us
  starting transfers between devices: 8.78 us -> 16.8 us
    all_gather x2 -> x0, waiting for transfers between devices: 70.5 us -> none  [body(): lax.all_gather(panel_part.astype(jnp.bfloat16), 'region', axis=0, tiled=T...]
    ppermute x0 -> x4, waiting for transfers between devices: none -> 59.5 us  [get_node(): lax.ppermute(arr_out, axis_name='region', perm=[(ii, (ii - fresh) % reply...]
    ppermute x0 -> x4, starting transfers between devices: none -> 8.27 us  [get_node(): lax.ppermute(arr_out, axis_name='region', perm=[(ii, (ii - fresh) % reply...]
  transfers between devices with their start and end apart: 6 -> 8, of which waited for: 5 -> 7; matrix products, arithmetic and copies ran while one was open for 1% -> 1% of each run, Pallas kernels for 0% -> 0%
where the time goes in v1:
time: 653 us; the launch traced here: 645 us
  local copies, waits for them, and re-layouts  237 us (36%)
  waiting for transfers between devices  180 us (28%)
  other arithmetic  135 us (21%)
  matrix products  33.8 us (5%)
  blocking collectives  28.2 us (4%)
  starting transfers between devices  16.8 us (3%)
  between operations  14 us (2%)
    convert_element_type x2, local copies, waits for them, and re-layouts, placed(): summed.astype(jnp.bfloat16).reshape(blocks.shape[0] * 8, pose_count * 8)  213 us
    psum x2, waiting for transfers between devices, broadcast(): return lax.psum(block, axis)  117 us
    convert_element_type x2, other arithmetic, placed(): summed.astype(jnp.bfloat16).reshape(blocks.shape[0] * 8, pose_count * 8)  66.7 us
    ppermute x4, waiting for transfers between devices, get_node(): lax.ppermute(arr_out, axis_name='region', perm=[(ii, (ii - fresh) % reply...  59.5 us
    another operation x6, other arithmetic, body(): factor = jnp.tril(jnp.linalg.cholesky(diagonal))  24.9 us
    another operation x4, other arithmetic, finish(): jax.scipy.linalg.solve_triangular(factor, block_rows.T, lower=True)  21 us
    dot_general x2, matrix products, body(): matrix = matrix - jnp.dot(mine, theirs.T, precision=lax.Precision.HIGHEST)  18.5 us
    all_gather x1, blocking collectives, body(): piece_labels = lax.all_gather(arrived_labels, 'col', axis=0, tiled=True)  14.2 us
  transfers between devices with their start and end apart: 8, of which 7 were waited for; matrix products, arithmetic and copies ran while one was open for 1% of the time, Pallas kernels for 0%

profile of v1, /device:TPU:0, one launch (start us, length us, event | category | flops | bytes accessed | tf_op | source)
XLA Modules:
  0.0 644.7 jit_solution(12703639742497361199)
XLA Ops:
  10.1 5.2 all-to-all-start
  16.0 3.9 all-to-all-done
  19.9 3.2 all-to-all-start.1
  23.4 14.2 %all_gather.6 = bf16[32,6,6]{2,1,0:T(8,128)(2,1)S(1)} all-gather(bf16[4,6,6]{2,1,0:T(8,128)(2,1)S(1)} %copy.35), channel_id=1, replica_groups=mesh['region'=4,'col'=8] {'col'}, dimensions={0}, use_global_device_ids=true | all-gather | bytes 2592 | tf_op jit(solution)/shard_map/all_gather | solution.py:86
  38.9 14.0 %all_gather.7 = bf16[32,6,128]{2,1,0:T(8,128)(2,1)S(1)} all-gather(bf16[4,6,128]{2,1,0:T(8,128)(2,1)S(1)} %all-to-all-done.1), channel_id=1, replica_groups=mesh['region'=4,'col'=8] {'col'}, dimensions={0}, use_global_device_ids=true | all-gather | bytes 55296 | tf_op jit(solution)/shard_map/all_gather | solution.py:85
  52.9 0.8 reshape.294
  53.8 43.1 %add_convert_fusion = bf16[192,8,256,8]{3,2,1,0:T(8,128)(2,1)} fusion(f32[192,8,8]{2,1,0:T(8,128)S(1)} %get-tuple-element.34, f32[192,256]{1,0:T(8,128)S(1)} %get-tuple-element.38, f32[192,8,8]{2,1,0:T(8,128)S(1)} %get-tuple-element.33, f32[192,256]{1,0:T(8,128)S(1)} %get-tuple-element.37), kind=kLoop, calls=%fused_computation | loop fusion | flops 12582912 | bytes 6782976 | tf_op jit(solution)/shard_map/convert_element_type | solution.py:46
  96.9 141.8 %convert_element_type.99 = bf16[1536,2048]{1,0:T(8,128)(2,1)} reshape(bf16[192,8,256,8]{3,2,1,0:T(8,128)(2,1)} %add_convert_fusion) | data formatting | bytes 12582912 | tf_op jit(solution)/shard_map/convert_element_type | solution.py:46
  238.7 23.6 %add_convert_fusion.1 = bf16[192,8,128,8]{3,2,1,0:T(8,128)(2,1)} fusion(f32[192,8,8]{2,1,0:T(8,128)S(1)} %get-tuple-element.34, f32[192,128]{1,0:T(8,128)S(1)} %copy-done.9, f32[192,8,8]{2,1,0:T(8,128)S(1)} %get-tuple-element.33, f32[192,128]{1,0:T(8,128)S(1)} %copy-done.8), kind=kLoop, calls=%fused_computation.1 | loop fusion | flops 6291456 | bytes 3440640 | tf_op jit(solution)/shard_map/convert_element_type | solution.py:46
  262.3 71.0 %convert_element_type.103 = bf16[1536,1024]{1,0:T(8,128)(2,1)S(1)} reshape(bf16[192,8,128,8]{3,2,1,0:T(8,128)(2,1)} %add_convert_fusion.1) | data formatting | bytes 6291456 | tf_op jit(solution)/shard_map/convert_element_type | solution.py:46
  333.3 9.5 %select_add_fusion = f32[2048,1024]{0,1:T(8,128)S(1)} fusion(f32[2048]{0:T(1024)S(1)} %copy-done.10, s32[2048]{0:T(1024)S(1)} %iota_add_fusion, s32[1024]{0:T(1024)S(1)} %iota_add_fusion.1, bf16[1536,2048]{1,0:T(8,128)(2,1)} %convert_element_type.99, bf16[1536,1024]{1,0:T(8,128)(2,1)S(1)} %convert_element_type.103), kind=kOutput, calls=%fused_computation.2 | convolution fusion | flops 6448742400 | bytes 17846272 | tf_op jit(solution)/shard_map/dot_general | solution.py:94
  342.8 3.4 copy-done.3
  347.1 58.0 %all-reduce.3.cloned.1.call-done = bf16[2048,128]{0,1:T(8,128)(2,1)} async-done(((bf16[2048,128]{0,1:T(8,128)(2,1)}), bf16[2048,128]{0,1:T(8,128)(2,1)}) %all-reduce.3.cloned.1.call-update) | async-done | bytes 524304 | tf_op jit(solution)/shard_map/psum | solution.py:37
  405.1 2.8 collective-permute-start
  407.9 9.7 %collective-permute-done = bf16[2048,128]{0,1:T(8,128)(2,1)S(1)} collective-permute-done((bf16[2048,128]{0,1:T(8,128)(2,1)}, bf16[2048,128]{0,1:T(8,128)(2,1)S(1)}, u32[]{:S(2)}, u32[]{:S(2)}) %collective-permute-start) | collective-permute-done | bytes 524320 | tf_op jit(solution)/shard_map/ppermute | solution.py:20
  417.7 1.1 pad_maximum_fusion
  418.8 1.5 collective-permute-start.1
  421.0 20.1 %collective-permute-done.1 = bf16[4096,128]{0,1:T(8,128)(2,1)S(1)} collective-permute-done((bf16[4096,128]{0,1:T(8,128)(2,1)S(1)}, bf16[4096,128]{0,1:T(8,128)(2,1)S(1)}, u32[]{:S(2)}, u32[]{:S(2)}) %collective-permute-start.1) | collective-permute-done | bytes 1048608 | tf_op jit(solution)/shard_map/ppermute | solution.py:20
  441.1 3.0 fusion.11
  444.2 1.9 copy-done.5
  446.2 0.9 fusion.37
  447.1 11.7 %cholesky.44 = f32[128,128]{1,0:T(8,128)S(1)} custom-call(f32[128,128]{1,0:T(8,128)S(1)} %fusion.37), custom_call_target="Cholesky" | custom-call | tf_op jit(solution)/shard_map/jit(cholesky)/cholesky | solution.py:114
  460.2 9.8 %custom-call.10 = f32[1,128,128]{1,2,0:T(8,128)S(1)} custom-call(f32[1,128,128]{2,1,0:T(8,128)S(1)} %fusion.30), custom_call_target="InvertDiagBlocksLowerTriangular" | custom-call | tf_op jit(solution)/shard_map/jit(_solve_triangular)/triangular_solve | solution.py:118
  470.0 1.7 fusion.15
  471.7 1.1 fusion.1
  472.8 9.2 %convolution_subtract_fusion.1 = f32[2048,1024]{0,1:T(8,128)S(1)} fusion(f32[2048,1024]{0,1:T(8,128)} %copy-done.3, f32[2048,128]{0,1:T(8,128)S(1)} %fusion.1, f32[1024,128]{0,1:T(8,128)S(1)} %fusion.15), kind=kOutput, calls=%fused_computation.6 | convolution fusion | flops 3223322624 | bytes 18350080 | tf_op jit(solution)/shard_map/dot_general | solution.py:124
  482.0 0.9 fusion.16
  482.9 0.9 and_select_fusion
  483.9 3.4 copy-done.2
  487.2 0.8 fusion.23
  488.1 58.6 %all-reduce.5.cloned.1.call-done = bf16[2048,128]{0,1:T(8,128)(2,1)} async-done(((bf16[2048,128]{0,1:T(8,128)(2,1)}), bf16[2048,128]{0,1:T(8,128)(2,1)}) %all-reduce.5.cloned.1.call-update) | async-done | bytes 524304 | tf_op jit(solution)/shard_map/psum | solution.py:37
  546.7 2.4 collective-permute-start.2
  549.1 9.7 %collective-permute-done.2 = bf16[2048,128]{0,1:T(8,128)(2,1)S(1)} collective-permute-done((bf16[2048,128]{0,1:T(8,128)(2,1)}, bf16[2048,128]{0,1:T(8,128)(2,1)S(1)}, u32[]{:S(2)}, u32[]{:S(2)}) %collective-permute-start.2) | collective-permute-done | bytes 524320 | tf_op jit(solution)/shard_map/ppermute | solution.py:20
  558.8 1.1 pad_maximum_fusion.1
  559.9 1.5 collective-permute-start.3
  561.5 0.9 compare_reduce_fusion.2
  562.3 19.9 %collective-permute-done.3 = bf16[4096,128]{0,1:T(8,128)(2,1)S(1)} collective-permute-done((bf16[4096,128]{0,1:T(8,128)(2,1)S(1)}, bf16[4096,128]{0,1:T(8,128)(2,1)S(1)}, u32[]{:S(2)}, u32[]{:S(2)}) %collective-permute-start.3) | collective-permute-done | bytes 1048608 | tf_op jit(solution)/shard_map/ppermute | solution.py:20
  582.3 3.0 fusion.5
  585.3 1.9 copy-done.4
  587.3 0.9 fusion.34
  588.2 11.7 %cholesky.55 = f32[128,128]{1,0:T(8,128)S(1)} custom-call(f32[128,128]{1,0:T(8,128)S(1)} %fusion.34), custom_call_target="Cholesky" | custom-call | tf_op jit(solution)/shard_map/jit(cholesky)/cholesky | solution.py:114
  601.3 9.8 %custom-call.12 = f32[1,128,128]{1,2,0:T(8,128)S(1)} custom-call(f32[1,128,128]{2,1,0:T(8,128)S(1)} %fusion.31), custom_call_target="InvertDiagBlocksLowerTriangular" | custom-call | tf_op jit(solution)/shard_map/jit(_solve_triangular)/triangular_solve | solution.py:118
  611.1 1.7 fusion.14
  612.8 1.1 fusion
  613.9 9.4 %convolution_subtract_fusion = f32[2048,1024]{0,1:T(8,128)S(1)} fusion(f32[2048,1024]{0,1:T(8,128)} %copy-done.2, f32[2048,128]{0,1:T(8,128)S(1)} %fusion, f32[1024,128]{0,1:T(8,128)S(1)} %fusion.14), kind=kOutput, calls=%fused_computation.5 | convolution fusion | flops 3223322624 | bytes 18350080 | tf_op jit(solution)/shard_map/dot_general | solution.py:124
  623.3 0.9 fusion.17
  624.2 4.1 and_select_fusion.1
  628.4 9.3 %copy.43 = f32[2048,1024]{1,0:T(8,128)} copy(f32[2048,1024]{0,1:T(8,128)} %and_select_fusion.1) | data formatting | bytes 16777216 | tf_op jit(solution)/shard_map/jit(_where)/select_n | solution.py:129
  (71 shorter events, 10.6 us)
Async XLA Ops:
  6.5 8.7 %copy-start = (bf16[8,128]{1,0:T(8,128)(2,1)S(1)}, bf16[8,128]{1,0:T(8,128)(2,1)}, u32[]{:S(2)}) copy-start(bf16[8,128]{1,0:T(8,128)(2,1)} %param.15) | copy-start | bytes 6148
  10.1 9.9 %all-to-all-start = ((bf16[4,6,6]{1,2,0:T(8,128)(2,1)}), bf16[4,6,6]{1,2,0:T(8,128)(2,1)S(1)}, u32[]{:S(2)}, u32[]{:S(2)}) async-start(bf16[4,6,6]{1,2,0:T(8,128)(2,1)} %copy.34), calls=%async_computation | async-start | bytes 16384 | tf_op jit(solution)/shard_map/all_to_all | solution.py:83
  19.9 19.0 %all-to-all-start.1 = ((bf16[4,6,128]{2,1,0:T(8,128)(2,1)}), bf16[4,6,128]{2,1,0:T(8,128)(2,1)S(1)}, u32[]{:S(2)}, u32[]{:S(2)}) async-start(bf16[4,6,128]{2,1,0:T(8,128)(2,1)} %reshape.292), calls=%async_computation.1 | async-start | bytes 16384 | tf_op jit(solution)/shard_map/all_to_all | solution.py:82
  23.2 381.9 %all-reduce.3.cloned.1.call-start = ((), (), s32[]{:S(2)}) async-start(), calls=%async_computation.2 | async-start | bytes 1048576 | tf_op jit(solution)/shard_map/psum | solution.py:37
  96.9 141.8 %copy-start.8 = (f32[192,128]{1,0:T(8,128)S(1)}, f32[192,128]{1,0:T(8,128)}, u32[]{:S(2)}) copy-start(f32[192,128]{1,0:T(8,128)} %get-tuple-element.41) | copy-start | bytes 294916
  96.9 141.8 %copy-start.9 = (f32[192,128]{1,0:T(8,128)S(1)}, f32[192,128]{1,0:T(8,128)}, u32[]{:S(2)}) copy-start(f32[192,128]{1,0:T(8,128)} %get-tuple-element.42) | copy-start | bytes 294916
  262.3 71.0 %copy-start.10 = (f32[2048]{0:T(1024)S(1)}, f32[2048]{0:T(1024)}, u32[]{:S(2)}) copy-start(f32[2048]{0:T(1024)} %param.18) | copy-start | bytes 24580
  342.8 3.4 copy-start.3
  347.1 199.6 %all-reduce.5.cloned.1.call-start = ((), (), s32[]{:S(2)}) async-start(), calls=%async_computation.3 | async-start | bytes 1048576 | tf_op jit(solution)/shard_map/psum | solution.py:37
  405.1 12.5 %collective-permute-start = (bf16[2048,128]{0,1:T(8,128)(2,1)}, bf16[2048,128]{0,1:T(8,128)(2,1)S(1)}, u32[]{:S(2)}, u32[]{:S(2)}) collective-permute-start(bf16[2048,128]{0,1:T(8,128)(2,1)} %all-reduce.3.cloned.1.call-done), channel_id=1, source_target_pairs={{0,24},{8,0},{16,8},{24,16},{1,25},{9,1},{17,9},{25,17},{2,26},{10... | collective-permute-start | bytes 1572872 | tf_op jit(solution)/shard_map/ppermute | solution.py:20
  418.8 52.9 %copy-start.6 = (bf16[2048,128]{0,1:T(8,128)(2,1)S(1)}, bf16[2048,128]{0,1:T(8,128)(2,1)}, u32[]{:S(2)}) copy-start(bf16[2048,128]{0,1:T(8,128)(2,1)} %all-reduce.3.cloned.1.call-done) | copy-start | bytes 1572868
  418.8 22.3 %collective-permute-start.1 = (bf16[4096,128]{0,1:T(8,128)(2,1)S(1)}, bf16[4096,128]{0,1:T(8,128)(2,1)S(1)}, u32[]{:S(2)}, u32[]{:S(2)}) collective-permute-start(bf16[4096,128]{0,1:T(8,128)(2,1)S(1)} %pad_maximum_fusion), channel_id=1, source_target_pairs={{0,16},{8,24},{16,0},{24,8},{1,17},{9,25},{17,1},{25,9},{2,18},{10... | collective-permute-start | bytes 3145736 | tf_op jit(solution)/shard_map/ppermute | solution.py:20
  444.2 1.9 copy-start.5
  483.8 3.4 copy-start.2
  546.7 12.1 %collective-permute-start.2 = (bf16[2048,128]{0,1:T(8,128)(2,1)}, bf16[2048,128]{0,1:T(8,128)(2,1)S(1)}, u32[]{:S(2)}, u32[]{:S(2)}) collective-permute-start(bf16[2048,128]{0,1:T(8,128)(2,1)} %all-reduce.5.cloned.1.call-done), channel_id=1, source_target_pairs={{0,24},{8,0},{16,8},{24,16},{1,25},{9,1},{17,9},{25,17},{2,26},{10... | collective-permute-start | bytes 1572872 | tf_op jit(solution)/shard_map/ppermute | solution.py:20
  559.9 52.9 %copy-start.7 = (bf16[2048,128]{0,1:T(8,128)(2,1)S(1)}, bf16[2048,128]{0,1:T(8,128)(2,1)}, u32[]{:S(2)}) copy-start(bf16[2048,128]{0,1:T(8,128)(2,1)} %all-reduce.5.cloned.1.call-done) | copy-start | bytes 1572868
  559.9 22.3 %collective-permute-start.3 = (bf16[4096,128]{0,1:T(8,128)(2,1)S(1)}, bf16[4096,128]{0,1:T(8,128)(2,1)S(1)}, u32[]{:S(2)}, u32[]{:S(2)}) collective-permute-start(bf16[4096,128]{0,1:T(8,128)(2,1)S(1)} %pad_maximum_fusion.1), channel_id=1, source_target_pairs={{0,16},{8,24},{16,0},{24,8},{1,17},{9,25},{17,1},{25,9},{2,18},{10... | collective-permute-start | bytes 3145736 | tf_op jit(solution)/shard_map/ppermute | solution.py:20
  585.3 1.9 copy-start.4
  628.3 9.3 %copy-start.1 = (bf16[8,128]{1,0:T(8,128)(2,1)S(1)}, bf16[8,128]{1,0:T(8,128)(2,1)}, u32[]{:S(2)}) copy-start(bf16[8,128]{1,0:T(8,128)(2,1)} %param.15) | copy-start | bytes 6148
Sparse Core Ops, SparseCore 0:
  347.2 57.8 all-reduce.2
  488.2 58.4 all-reduce.4
